TPU v7x, 256 devices: a whole 4x4x8 slice. The times are simulated.
256 devices in a mesh: row: 8 (over x, core), col: 32 (over z, y).
Axes of the slice: x: 4, y: 4, z: 8, core: 2. Of those that a mesh axis runs over, the one named last changes fastest.
Arguments:
- ancestor_order: int32 [2, 48], replicated, may hold values from 0 to 47, each once within a row
- factor_rows: bfloat16 [2, 24576, 512], P(None, ('row', 'col')), may hold values from -0.0390625 to 0.0390625
- factor_inverse: bfloat16 [2, 512, 512], replicated
- ancestor_inverse: bfloat16 [24576, 24576], P('col', 'row'), may hold values from -6 to 6
- diagonal_inverse: float32 [2, 512, 512], P(None, None, 'row'), may hold values from -6 to 6
Outputs:
- offdiag_inverse: bfloat16 [2, 24576, 512], P(None, 'col', 'row')
- diag_updated: float32 [2, 512, 512], P(None, None, 'row')
Inputs may be any that keep to these rules, and one draw needn't show every extreme that they name: `ancestor_order`: each row lists every ancestor block once; its first 40 entries are the blocks coupled to that supernode.
All inputs are finite; a program needn't handle non-finite values.
Results may differ from a plain program's by a relative error of at most 0.011.
Values may be sent and summed in bfloat16 or wider, within the bound.
No kernel may reach another device: no remote copies, remote signals or barrier semaphores. Data moves between devices by JAX's collectives and lax.ppermute only.
A program may use at most 128 MiB of HBM per device.

v0:
```python
import jax
import jax.numpy as jnp
from jax import lax
from jax.sharding import Mesh
from jax.sharding import PartitionSpec as P

NSEL = 40
XS, CORES, ZS, YS = (4, 2, 8, 4)
ROW = ("x", "core")
COL = ("z", "y")
ALL = ("x", "core", "z", "y")
F32 = jnp.float32
BF16 = jnp.bfloat16


def shift(array, axis, size, by):
    return lax.ppermute(array, axis, [(i, (i + by) % size) for i in range(size)])


def direct_ring(array, axis, size):
    return [array] + [
        shift(array, axis, size, d if d <= size // 2 else d - size) for d in range(1, size)
    ]


def relay_ring(array, axis, size, halved):
    got = [array] + [None] * (size - 1)
    right = left = array
    for step in range(1, size // 2):
        right = shift(right, axis, size, 1)
        left = shift(left, axis, size, -1)
        got[step], got[size - step] = (right, left)
    if halved:
        half = array.shape[0] // 2
        got[size // 2] = jnp.concatenate(
            [shift(right[:half], axis, size, 1), shift(left[half:], axis, size, -1)], axis=0
        )
    else:
        got[size // 2] = shift(right, axis, size, 1)
    return got


def placed_by_owner(got, own, axis):
    size, width = (len(got), got[0].shape[axis])
    dims = list(got[0].shape)
    dims[axis] *= size
    whole = jnp.zeros(dims, got[0].dtype)
    for d, chunk in enumerate(got):
        whole = lax.dynamic_update_slice_in_dim(whole, chunk, (own - d) % size * width, axis)
    return whole


def panel_y_then_z(piece):
    part = placed_by_owner(direct_ring(piece, "y", YS), lax.axis_index("y"), 0)
    return lax.all_gather(part, "z", axis=0, tiled=True)


def near_z_then_y(piece):
    part = placed_by_owner(relay_ring(piece[None], "z", ZS, False), lax.axis_index("z"), 0)[:, None]
    return [part, shift(part, "y", YS, 1), shift(part, "y", YS, -1)]


def far_chunk(near):
    half = near[0].shape[0] // 2
    right = shift(near[1][:half], "y", YS, 1)
    return jnp.concatenate([right, shift(near[2][half:], "y", YS, -1)], axis=0)


def device(x, core, z, y):
    return ((x * CORES + core) * ZS + z) * YS + y


def root_of(z):
    return (z // CORES, z % CORES)


def from_root(array, target):
    pairs = []
    for z in range(ZS):
        for y in range(YS):
            x, core = root_of(z)
            pairs.append((device(x, core, z, y), device(*target(x, core, z, y))))
    return lax.ppermute(array, ALL, pairs)


def along_x(slab, core, shifts):
    return sum((from_root(slab, lambda x, c, z, y: ((x + by) % XS, core, z, y)) for by in shifts))


def pair_sum(partial):
    first = lax.axis_index("core") == 0
    given = lax.ppermute(jnp.where(first, partial[1], partial[0]), "core", [(0, 1), (1, 0)])
    pair = jnp.where(first, partial[0], partial[1]).astype(F32) + given.astype(F32)
    return pair.astype(BF16)


def sum_over_x(pair):
    x = lax.axis_index("x")
    pair = pair.reshape(XS, -1, pair.shape[1])
    tile = lambda k: lax.dynamic_index_in_dim(pair, (x + k) % XS, 0, keepdims=False)
    opposite = shift(tile(2), "x", XS, 2)
    near = shift(tile(1), "x", XS, 1).astype(F32) + shift(tile(3), "x", XS, -1).astype(F32)
    return tile(0).astype(F32) + opposite.astype(F32) + near


def exchanged(array, axis, size, by):
    return lax.ppermute(array, axis, [(i, i ^ by) for i in range(size)])


def summed_over_col(array):
    y = lax.axis_index("y")
    quarters = array.reshape(YS, -1, array.shape[1])
    own = lambda k: lax.dynamic_index_in_dim(quarters, y ^ k, 0, keepdims=False)
    part = own(0).astype(F32)
    for k in range(1, YS):
        part = part + exchanged(own(k), "y", YS, k).astype(F32)
    part = lax.optimization_barrier(part.astype(BF16))
    copies = jnp.broadcast_to(part[None], (ZS, *part.shape))
    part = lax.all_to_all(copies, "z", split_axis=0, concat_axis=0, tiled=True)
    part = lax.optimization_barrier(part.astype(F32).sum(axis=0).astype(BF16))
    whole = jnp.zeros(quarters.shape, BF16)
    for k in range(YS):
        got = part if k == 0 else exchanged(part, "y", YS, k)
        whole = lax.dynamic_update_slice_in_dim(whole, got[None], y ^ k, 0)
    return whole.reshape(array.shape)


def own_slab_of_both(array):
    core = lax.axis_index("core")
    slabs = array.reshape(CORES, -1, array.shape[1])
    kept = lax.dynamic_index_in_dim(slabs, core, 0, keepdims=False)
    given = lax.dynamic_index_in_dim(slabs, 1 - core, 0, keepdims=False)
    got = lax.ppermute(given, "core", [(0, 1), (1, 0)])
    return jnp.stack([jnp.where(core == 0, kept, got), jnp.where(core == 0, got, kept)])


def body(listing, pieces, factor_inv, inverse_block, diag_inv):
    piece_rows, width = pieces.shape[1:]
    row = lax.axis_index(ROW)
    col = lax.axis_index(COL)
    core, z, y = (lax.axis_index("core"), lax.axis_index("z"), lax.axis_index("y"))
    chosen = listing[:, :NSEL]

    def keep_of(first, count):
        labels = (first + jnp.arange(count, dtype=jnp.int32)) // width
        return jnp.any(chosen[:, :, None] == labels[None, None, :], axis=1).astype(F32)

    own_keep = keep_of((row * ZS * YS + col) * piece_rows, piece_rows)
    normed = jnp.einsum("srk,skj->srj", pieces, factor_inv, preferred_element_type=F32)
    normed = (normed * own_keep[:, :, None]).astype(BF16)
    rows = inverse_block.shape[0]

    def partial_of(panel):
        return jnp.einsum("qj,pq->jp", panel, inverse_block, preferred_element_type=F32).astype(
            BF16
        )

    first = core == 0
    near = near_z_then_y(normed[1])
    deep = rows // (piece_rows * YS)
    of_slab = lambda part, lane: lax.dynamic_slice_in_dim(part, lane * deep, deep, 0)
    far_part = from_root(of_slab(near[0], (y + 2) % YS), lambda x, c, z, y: (x, c, z, (y + 2) % YS))
    slab_parts = [of_slab(near[0], y), of_slab(near[1], y), far_part, of_slab(near[2], y)]
    slab_1 = placed_by_owner(slab_parts, y, 1).reshape(rows, width)
    sent_1 = along_x(slab_1, 1, (1, -1, -2))
    panel_0 = panel_y_then_z(normed[0])
    panel_0, near = lax.optimization_barrier((panel_0, near))
    chunks = [near[0], near[1], far_chunk(near), near[2]]
    slab_0 = lax.dynamic_slice_in_dim(panel_0, y * rows, rows, 0)
    sent_0 = along_x(slab_0, 0, (1, -1, 2))
    partial = [partial_of(panel_0)]
    chunks, partial[0] = lax.optimization_barrier((chunks, partial[0]))
    across = from_root(jnp.where(first, slab_1, slab_0), lambda x, c, z, y: (x, 1 - c, z, y))
    partial.append(partial_of(placed_by_owner(chunks, y, 1).reshape(panel_0.shape)))
    home = row == z
    factor_slab = jnp.where(home, jnp.where(first, slab_0, slab_1), sent_0 + sent_1 + across)
    pair, factor_slab = lax.optimization_barrier((pair_sum(partial), factor_slab))
    product = sum_over_x(pair)
    col_keep = lax.dynamic_index_in_dim(keep_of(col * rows, rows), core, 0)
    offdiag = lax.optimization_barrier((-(product * col_keep)).astype(BF16))
    term = -jnp.dot(offdiag, factor_slab, preferred_element_type=F32)
    correction = own_slab_of_both(summed_over_col(term.astype(BF16)))
    return (
        own_slab_of_both(offdiag).transpose(0, 2, 1),
        diag_inv + correction.astype(F32).transpose(0, 2, 1),
    )


def solution(mesh):
    torus = Mesh(mesh.devices.reshape(XS, CORES, ZS, YS), ALL)
    return jax.shard_map(
        body,
        mesh=torus,
        in_specs=(P(), P(None, ALL, None), P(), P(COL, ROW), P(None, None, ROW)),
        out_specs=(P(None, COL, ROW), P(None, None, ROW)),
        check_vma=False,
    )
```

profile of v0, /device:TPU:1, one launch (start us, length us, event | category | flops | bytes accessed | tf_op | source)
XLA Modules:
  0.0 166.6 jit_solution(9911630012255583256)
XLA Ops:
  8.4 1.2 fusion
  9.7 3.8 %collective-permute-start.1 = (bf16[96,512]{1,0:T(8,128)(2,1)S(1)}, bf16[96,512]{1,0:T(8,128)(2,1)S(1)}, u32[]{:S(2)}, u32[]{:S(2)}) collective-permute-start(bf16[96,512]{1,0:T(8,128)(2,1)S(1)} %get-tuple-element.36), channel_id=1, source_target_pairs={{0,2},{1,3},{2,0},{3,1},{4,6},{5,7},{6,4},{7,5},{8,10},{9,11},{10,... | collective-permute-start | bytes 294920 | tf_op jit(solution)/shard_map/ppermute | solution.py:17
  13.9 2.3 %collective-permute-start.2 = (bf16[96,512]{1,0:T(8,128)(2,1)S(1)}, bf16[96,512]{1,0:T(8,128)(2,1)S(1)}, u32[]{:S(2)}, u32[]{:S(2)}) collective-permute-start(bf16[96,512]{1,0:T(8,128)(2,1)S(1)} %get-tuple-element.36), channel_id=1, source_target_pairs={{0,3},{1,0},{2,1},{3,2},{4,7},{5,4},{6,5},{7,6},{8,11},{9,8},{10,9... | collective-permute-start | bytes 294920 | tf_op jit(solution)/shard_map/ppermute | solution.py:17
  16.3 3.8 %collective-permute-done = bf16[96,512]{1,0:T(8,128)(2,1)S(1)} collective-permute-done((bf16[96,512]{1,0:T(8,128)(2,1)S(1)}, bf16[96,512]{1,0:T(8,128)(2,1)S(1)}, u32[]{:S(2)}, u32[]{:S(2)}) %collective-permute-start) | collective-permute-done | bytes 98336 | tf_op jit(solution)/shard_map/ppermute | solution.py:17
  21.1 3.8 %collective-permute-start.7 = (bf16[1,96,512]{2,1,0:T(8,128)(2,1)S(1)}, bf16[1,96,512]{2,1,0:T(8,128)(2,1)S(1)}, u32[]{:S(2)}, u32[]{:S(2)}) collective-permute-start(bf16[1,96,512]{2,1,0:T(8,128)(2,1)S(1)} %get-tuple-element.35), channel_id=1, source_target_pairs={{0,28},{4,0},{8,4},{12,8},{16,12},{20,16},{24,20},{28,24},{1,29},{... | collective-permute-start | bytes 294920 | tf_op jit(solution)/shard_map/ppermute | solution.py:17
  25.1 1.7 %collective-permute-done.3 = bf16[1,96,512]{2,1,0:T(8,128)(2,1)S(1)} collective-permute-done((bf16[1,96,512]{2,1,0:T(8,128)(2,1)S(1)}, bf16[1,96,512]{2,1,0:T(8,128)(2,1)S(1)}, u32[]{:S(2)}, u32[]{:S(2)}) %collective-permute-start.3) | collective-permute-done | bytes 98336 | tf_op jit(solution)/shard_map/ppermute | solution.py:17
  26.8 2.8 %collective-permute-start.8 = (bf16[1,96,512]{2,1,0:T(8,128)(2,1)S(1)}, bf16[1,96,512]{2,1,0:T(8,128)(2,1)S(1)}, u32[]{:S(2)}, u32[]{:S(2)}) collective-permute-start(bf16[1,96,512]{2,1,0:T(8,128)(2,1)S(1)} %collective-permute-done.7), channel_id=1, source_target_pairs={{0,28},{4,0},{8,4},{12,8},{16,12},{20,16},{24,20},{28,24},{1,29},{... | collective-permute-start | bytes 294920 | tf_op jit(solution)/shard_map/ppermute | solution.py:17
  29.6 1.9 %collective-permute-done.4 = bf16[1,96,512]{2,1,0:T(8,128)(2,1)S(1)} collective-permute-done((bf16[1,96,512]{2,1,0:T(8,128)(2,1)S(1)}, bf16[1,96,512]{2,1,0:T(8,128)(2,1)S(1)}, u32[]{:S(2)}, u32[]{:S(2)}) %collective-permute-start.4) | collective-permute-done | bytes 98336 | tf_op jit(solution)/shard_map/ppermute | solution.py:17
  31.5 2.8 %collective-permute-start.9 = (bf16[1,96,512]{2,1,0:T(8,128)(2,1)S(1)}, bf16[1,96,512]{2,1,0:T(8,128)(2,1)S(1)}, u32[]{:S(2)}, u32[]{:S(2)}) collective-permute-start(bf16[1,96,512]{2,1,0:T(8,128)(2,1)S(1)} %collective-permute-done.8), channel_id=1, source_target_pairs={{0,28},{4,0},{8,4},{12,8},{16,12},{20,16},{24,20},{28,24},{1,29},{... | collective-permute-start | bytes 294920 | tf_op jit(solution)/shard_map/ppermute | solution.py:17
  34.3 1.9 %collective-permute-done.5 = bf16[1,96,512]{2,1,0:T(8,128)(2,1)S(1)} collective-permute-done((bf16[1,96,512]{2,1,0:T(8,128)(2,1)S(1)}, bf16[1,96,512]{2,1,0:T(8,128)(2,1)S(1)}, u32[]{:S(2)}, u32[]{:S(2)}) %collective-permute-start.5) | collective-permute-done | bytes 98336 | tf_op jit(solution)/shard_map/ppermute | solution.py:17
  36.2 7.8 %collective-permute-done.6 = bf16[1,96,512]{2,1,0:T(8,128)(2,1)S(1)} collective-permute-done((bf16[1,96,512]{2,1,0:T(8,128)(2,1)S(1)}, bf16[1,96,512]{2,1,0:T(8,128)(2,1)S(1)}, u32[]{:S(2)}, u32[]{:S(2)}) %collective-permute-start.6) | collective-permute-done | bytes 98336 | tf_op jit(solution)/shard_map/ppermute | solution.py:17
  44.1 1.9 %collective-permute-start.10 = (bf16[8,1,96,512]{3,2,1,0:T(8,128)(2,1)S(1)}, bf16[8,1,96,512]{3,2,1,0:T(8,128)(2,1)}, u32[]{:S(2)}, u32[]{:S(2)}) collective-permute-start(bf16[8,1,96,512]{3,2,1,0:T(8,128)(2,1)S(1)} %bitcast_dynamic-update-slice_fusion), channel_id=1, source_target_pairs={{0,1},{1,2},{2,3},{3,0},{4,5},{5,6},{6,7},{7,4},{8,9},{9,10},{10,1... | collective-permute-start | bytes 2359304 | tf_op jit(solution)/shard_map/ppermute | solution.py:17
  46.0 1.1 collective-permute-start.11
  47.9 1.3 collective-permute-start.15
  49.3 7.6 %collective-permute-done.10 = bf16[8,1,96,512]{3,2,1,0:T(8,128)(2,1)} collective-permute-done((bf16[8,1,96,512]{3,2,1,0:T(8,128)(2,1)S(1)}, bf16[8,1,96,512]{3,2,1,0:T(8,128)(2,1)}, u32[]{:S(2)}, u32[]{:S(2)}) %collective-permute-start.10) | collective-permute-done | bytes 786464 | tf_op jit(solution)/shard_map/ppermute | solution.py:17
  56.8 0.9 dynamic-slice_dynamic-update-slice_fusion.1
  57.8 1.0 constant_dynamic-update-slice_fusion
  58.9 1.6 collective-permute-start.20
  60.4 1.6 collective-permute-start.19
  62.0 1.6 collective-permute-start.21
  63.6 8.1 %all-gather.2.cloned.1.call-done = bf16[3072,512]{1,0:T(8,128)(2,1)} async-done(((bf16[384,512]{1,0:T(8,128)(2,1)}), bf16[3072,512]{1,0:T(8,128)(2,1)}) %all-gather.2.cloned.1.call-update) | async-done | bytes 3145744 | tf_op jit(solution)/shard_map/all_gather | solution.py:55
  71.7 1.0 slice.18
  72.8 2.3 %collective-permute-start.13 = (bf16[4,1,96,512]{3,2,1,0:T(8,128)(2,1)S(1)}, bf16[4,1,96,512]{3,2,1,0:T(8,128)(2,1)S(1)}, u32[]{:S(2)}, u32[]{:S(2)}) collective-permute-start(bf16[4,1,96,512]{3,2,1,0:T(8,128)(2,1)S(1)} %slice.19), channel_id=1, source_target_pairs={{0,3},{1,0},{2,1},{3,2},{4,7},{5,4},{6,5},{7,6},{8,11},{9,8},{10,9... | collective-permute-start | bytes 1179656 | tf_op jit(solution)/shard_map/ppermute | solution.py:17
  75.1 5.9 %convolution_convert_fusion.1 = bf16[512,768]{1,0:T(8,128)(2,1)S(1)} fusion(bf16[3072,512]{1,0:T(8,128)(2,1)} %all-gather.2.cloned.1.call-done, bf16[768,3072]{1,0:T(8,128)(2,1)} %param.8), kind=kOutput, calls=%fused_computation.2 | convolution fusion | flops 2416312320 | bytes 8650752 | tf_op jit(solution)/shard_map/qj,pq->jp/dot_general | solution.py:154
  81.1 2.6 %broadcast_select_fusion = (bf16[768,512]{1,0:T(8,128)(2,1)}, bf16[768,512]{1,0:T(8,128)(2,1)S(1)}) fusion(pred[]{:T(512)S(6)} %eq.63, bf16[2,4,96,512]{3,2,1,0:T(8,128)(2,1)S(1)} %dynamic-slice_dynamic-update-slice_fusion, bf16[3072,512]{1,0:T(8,128)(2,1)} %all-gather.2.cloned.1.call-done, s32[]{:T(128)S(6)} %select_n.299), kind=kLoop, calls=%fused_computation.9 | loop fusion | flops 393216 | bytes 3145733 | tf_op jit(solution)/shard_map/jit(_where)/select_n | solution.py:173
  83.7 1.6 collective-permute-start.18
  85.3 1.6 collective-permute-start.17
  87.3 1.3 constant_dynamic-update-slice_fusion.3
  88.8 1.6 collective-permute-start.16
  90.4 1.3 collective-permute-start.22
  91.7 3.8 %broadcast_select_fusion.1 = (bf16[512,768]{1,0:T(8,128)(2,1)}, bf16[512,768]{1,0:T(8,128)(2,1)}) fusion(bf16[512,768]{1,0:T(8,128)(2,1)S(1)} %convolution_convert_fusion.1, pred[]{:T(512)S(6)} %eq.63, bf16[3072,512]{1,0:T(8,128)(2,1)S(1)} %bitcast.96, bf16[768,3072]{1,0:T(8,128)(2,1)S(1)} %bitcast.108), kind=kOutput, calls=%fused_computation.10 | convolution fusion | flops 2416705536 | bytes 10223617 | tf_op jit(solution)/shard_map/qj,pq->jp/dot_general | solution.py:154
  95.5 7.2 %collective-permute-start.14 = (bf16[512,768]{1,0:T(8,128)(2,1)}, bf16[512,768]{1,0:T(8,128)(2,1)}, u32[]{:S(2)}, u32[]{:S(2)}) collective-permute-start(bf16[512,768]{1,0:T(8,128)(2,1)} %get-tuple-element.40), channel_id=1, source_target_pairs={{0,32},{32,0},{1,33},{33,1},{2,34},{34,2},{3,35},{35,3},{4,36},{36... | collective-permute-start | bytes 2359304 | tf_op jit(solution)/shard_map/ppermute | solution.py:92
  102.7 2.7 %add_select_fusion = bf16[768,512]{1,0:T(8,128)(2,1)S(1)} fusion(bf16[768,512]{1,0:T(8,128)(2,1)S(1)} %collective-permute-done.22, bf16[768,512]{1,0:T(8,128)(2,1)} %collective-permute-done.21, bf16[768,512]{1,0:T(8,128)(2,1)} %collective-permute-done.19, bf16[768,512]{1,0:T(8,128)(2,1)} %collective-permute-done.20, ...), kind=kLoop, calls=%fused_computation.8 | loop fusion | flops 3145728 | bytes 7864322 | tf_op jit(solution)/shard_map/jit(_where)/select_n | solution.py:176
  105.5 1.4 add_convert_fusion
  107.2 1.5 collective-permute-start.24
  108.8 4.4 %collective-permute-done.23 = bf16[128,768]{1,0:T(8,128)(2,1)S(1)} collective-permute-done((bf16[128,768]{1,0:T(8,128)(2,1)S(1)}, bf16[128,768]{1,0:T(8,128)(2,1)S(1)}, u32[]{:S(2)}, u32[]{:S(2)}) %collective-permute-start.23) | collective-permute-done | bytes 196640 | tf_op jit(solution)/shard_map/ppermute | solution.py:17
  113.2 2.0 %collective-permute-done.24 = bf16[128,768]{1,0:T(8,128)(2,1)S(1)} collective-permute-done((bf16[128,768]{1,0:T(8,128)(2,1)S(1)}, bf16[128,768]{1,0:T(8,128)(2,1)S(1)}, u32[]{:S(2)}, u32[]{:S(2)}) %collective-permute-start.24) | collective-permute-done | bytes 196640 | tf_op jit(solution)/shard_map/ppermute | solution.py:17
  116.6 1.8 %collective-permute-start.29 = (bf16[32,512]{1,0:T(8,128)(2,1)S(1)}, bf16[32,512]{1,0:T(8,128)(2,1)S(1)}, u32[]{:S(2)}, u32[]{:S(2)}) collective-permute-start(bf16[32,512]{1,0:T(8,128)(2,1)S(1)} %get-tuple-element.38), channel_id=1, source_target_pairs={{0,3},{1,2},{2,1},{3,0},{4,7},{5,6},{6,5},{7,4},{8,11},{9,10},{10,... | collective-permute-start | bytes 98312 | tf_op jit(solution)/shard_map/ppermute | solution.py:107
  118.4 1.1 collective-permute-start.28
  119.5 1.1 collective-permute-done.29
  120.5 2.1 %collective-permute-done.28 = bf16[32,512]{1,0:T(8,128)(2,1)S(1)} collective-permute-done((bf16[32,512]{1,0:T(8,128)(2,1)S(1)}, bf16[32,512]{1,0:T(8,128)(2,1)S(1)}, u32[]{:S(2)}, u32[]{:S(2)}) %collective-permute-start.28) | collective-permute-done | bytes 32800 | tf_op jit(solution)/shard_map/ppermute | solution.py:107
  123.4 11.4 %all-to-all-start = ((bf16[8,32,512]{2,1,0:T(8,128)(2,1)}), bf16[8,32,512]{2,1,0:T(8,128)(2,1)S(1)}, u32[]{:S(2)}, u32[]{:S(2)}) async-start(bf16[8,32,512]{2,1,0:T(8,128)(2,1)} %broadcast_in_dim.68), calls=%async_computation | async-start | bytes 524288 | tf_op jit(solution)/shard_map/all_to_all | solution.py:119
  134.8 4.1 %collective-permute-start.26 = (bf16[64,768]{1,0:T(8,128)(2,1)S(1)}, bf16[64,768]{1,0:T(8,128)(2,1)S(1)}, u32[]{:S(2)}, u32[]{:S(2)}) collective-permute-start(bf16[64,768]{1,0:T(8,128)(2,1)S(1)} %dynamic-slice_bitcast_fusion.3), channel_id=1, source_target_pairs={{0,32},{32,0},{1,33},{33,1},{2,34},{34,2},{3,35},{35,3},{4,36},{36... | collective-permute-start | bytes 294920 | tf_op jit(solution)/shard_map/ppermute | solution.py:133
  138.8 0.9 collective-permute-done.26
  139.8 4.3 %all-to-all-done = bf16[8,32,512]{2,1,0:T(8,128)(2,1)S(1)} async-done(((bf16[8,32,512]{2,1,0:T(8,128)(2,1)}), bf16[8,32,512]{2,1,0:T(8,128)(2,1)S(1)}, u32[]{:S(2)}, u32[]{:S(2)}) %all-to-all-start) | async-done | bytes 262176 | tf_op jit(solution)/shard_map/all_to_all | solution.py:119
  144.5 2.2 %collective-permute-start.31 = (bf16[32,512]{1,0:T(8,128)(2,1)S(1)}, bf16[32,512]{1,0:T(8,128)(2,1)S(1)}, u32[]{:S(2)}, u32[]{:S(2)}) collective-permute-start(bf16[32,512]{1,0:T(8,128)(2,1)S(1)} %reduce_sum.12), channel_id=1, source_target_pairs={{0,2},{1,3},{2,0},{3,1},{4,6},{5,7},{6,4},{7,5},{8,10},{9,11},{10,... | collective-permute-start | bytes 98312 | tf_op jit(solution)/shard_map/ppermute | solution.py:107
  147.6 1.9 %collective-permute-done.30 = bf16[32,512]{1,0:T(8,128)(2,1)S(1)} collective-permute-done((bf16[32,512]{1,0:T(8,128)(2,1)S(1)}, bf16[32,512]{1,0:T(8,128)(2,1)S(1)}, u32[]{:S(2)}, u32[]{:S(2)}) %collective-permute-start.30) | collective-permute-done | bytes 32800 | tf_op jit(solution)/shard_map/ppermute | solution.py:107
  149.6 8.5 %collective-permute-start.33 = (bf16[64,512]{1,0:T(8,128)(2,1)S(1)}, bf16[64,512]{1,0:T(8,128)(2,1)S(1)}, u32[]{:S(2)}, u32[]{:S(2)}) collective-permute-start(bf16[64,512]{1,0:T(8,128)(2,1)S(1)} %dynamic-slice_bitcast_fusion.4), channel_id=1, source_target_pairs={{0,32},{32,0},{1,33},{33,1},{2,34},{34,2},{3,35},{35,3},{4,36},{36... | collective-permute-start | bytes 196616 | tf_op jit(solution)/shard_map/ppermute | solution.py:133
  (106 shorter events, 9.7 us)
Async XLA Ops:
  7.2 1.2 copy-start
  7.2 64.5 %all-gather.2.cloned.1.call-start = ((), (), s32[]{:S(2)}) async-start(), calls=%async_computation.1 | async-start | bytes 3538944 | tf_op jit(solution)/shard_map/all_gather | solution.py:55
  9.7 10.5 %collective-permute-start.1 = (bf16[96,512]{1,0:T(8,128)(2,1)S(1)}, bf16[96,512]{1,0:T(8,128)(2,1)S(1)}, u32[]{:S(2)}, u32[]{:S(2)}) collective-permute-start(bf16[96,512]{1,0:T(8,128)(2,1)S(1)} %get-tuple-element.36), channel_id=1, source_target_pairs={{0,2},{1,3},{2,0},{3,1},{4,6},{5,7},{6,4},{7,5},{8,10},{9,11},{10,... | collective-permute-start | bytes 294920 | tf_op jit(solution)/shard_map/ppermute | solution.py:17
  13.5 6.6 %collective-permute-start = (bf16[96,512]{1,0:T(8,128)(2,1)S(1)}, bf16[96,512]{1,0:T(8,128)(2,1)S(1)}, u32[]{:S(2)}, u32[]{:S(2)}) collective-permute-start(bf16[96,512]{1,0:T(8,128)(2,1)S(1)} %get-tuple-element.36), channel_id=1, source_target_pairs={{0,1},{1,2},{2,3},{3,0},{4,5},{5,6},{6,7},{7,4},{8,9},{9,10},{10,1... | collective-permute-start | bytes 294920 | tf_op jit(solution)/shard_map/ppermute | solution.py:17
  13.9 6.3 %collective-permute-start.2 = (bf16[96,512]{1,0:T(8,128)(2,1)S(1)}, bf16[96,512]{1,0:T(8,128)(2,1)S(1)}, u32[]{:S(2)}, u32[]{:S(2)}) collective-permute-start(bf16[96,512]{1,0:T(8,128)(2,1)S(1)} %get-tuple-element.36), channel_id=1, source_target_pairs={{0,3},{1,0},{2,1},{3,2},{4,7},{5,4},{6,5},{7,6},{8,11},{9,8},{10,9... | collective-permute-start | bytes 294920 | tf_op jit(solution)/shard_map/ppermute | solution.py:17
  20.2 0.7 copy-start.3
  21.0 5.9 %collective-permute-start.3 = (bf16[1,96,512]{2,1,0:T(8,128)(2,1)S(1)}, bf16[1,96,512]{2,1,0:T(8,128)(2,1)S(1)}, u32[]{:S(2)}, u32[]{:S(2)}) collective-permute-start(bf16[1,96,512]{2,1,0:T(8,128)(2,1)S(1)} %get-tuple-element.35), channel_id=1, source_target_pairs={{0,4},{4,8},{8,12},{12,16},{16,20},{20,24},{24,28},{28,0},{1,5},{5... | collective-permute-start | bytes 294920 | tf_op jit(solution)/shard_map/ppermute | solution.py:17
  21.1 5.8 %collective-permute-start.7 = (bf16[1,96,512]{2,1,0:T(8,128)(2,1)S(1)}, bf16[1,96,512]{2,1,0:T(8,128)(2,1)S(1)}, u32[]{:S(2)}, u32[]{:S(2)}) collective-permute-start(bf16[1,96,512]{2,1,0:T(8,128)(2,1)S(1)} %get-tuple-element.35), channel_id=1, source_target_pairs={{0,28},{4,0},{8,4},{12,8},{16,12},{20,16},{24,20},{28,24},{1,29},{... | collective-permute-start | bytes 294920 | tf_op jit(solution)/shard_map/ppermute | solution.py:17
  26.8 4.7 %collective-permute-start.4 = (bf16[1,96,512]{2,1,0:T(8,128)(2,1)S(1)}, bf16[1,96,512]{2,1,0:T(8,128)(2,1)S(1)}, u32[]{:S(2)}, u32[]{:S(2)}) collective-permute-start(bf16[1,96,512]{2,1,0:T(8,128)(2,1)S(1)} %collective-permute-done.3), channel_id=1, source_target_pairs={{0,4},{4,8},{8,12},{12,16},{16,20},{20,24},{24,28},{28,0},{1,5},{5... | collective-permute-start | bytes 294920 | tf_op jit(solution)/shard_map/ppermute | solution.py:17
  26.8 4.7 %collective-permute-start.8 = (bf16[1,96,512]{2,1,0:T(8,128)(2,1)S(1)}, bf16[1,96,512]{2,1,0:T(8,128)(2,1)S(1)}, u32[]{:S(2)}, u32[]{:S(2)}) collective-permute-start(bf16[1,96,512]{2,1,0:T(8,128)(2,1)S(1)} %collective-permute-done.7), channel_id=1, source_target_pairs={{0,28},{4,0},{8,4},{12,8},{16,12},{20,16},{24,20},{28,24},{1,29},{... | collective-permute-start | bytes 294920 | tf_op jit(solution)/shard_map/ppermute | solution.py:17
  31.5 4.7 %collective-permute-start.5 = (bf16[1,96,512]{2,1,0:T(8,128)(2,1)S(1)}, bf16[1,96,512]{2,1,0:T(8,128)(2,1)S(1)}, u32[]{:S(2)}, u32[]{:S(2)}) collective-permute-start(bf16[1,96,512]{2,1,0:T(8,128)(2,1)S(1)} %collective-permute-done.4), channel_id=1, source_target_pairs={{0,4},{4,8},{8,12},{12,16},{16,20},{20,24},{24,28},{28,0},{1,5},{5... | collective-permute-start | bytes 294920 | tf_op jit(solution)/shard_map/ppermute | solution.py:17
  31.5 12.6 %collective-permute-start.9 = (bf16[1,96,512]{2,1,0:T(8,128)(2,1)S(1)}, bf16[1,96,512]{2,1,0:T(8,128)(2,1)S(1)}, u32[]{:S(2)}, u32[]{:S(2)}) collective-permute-start(bf16[1,96,512]{2,1,0:T(8,128)(2,1)S(1)} %collective-permute-done.8), channel_id=1, source_target_pairs={{0,28},{4,0},{8,4},{12,8},{16,12},{20,16},{24,20},{28,24},{1,29},{... | collective-permute-start | bytes 294920 | tf_op jit(solution)/shard_map/ppermute | solution.py:17
  36.2 7.9 %collective-permute-start.6 = (bf16[1,96,512]{2,1,0:T(8,128)(2,1)S(1)}, bf16[1,96,512]{2,1,0:T(8,128)(2,1)S(1)}, u32[]{:S(2)}, u32[]{:S(2)}) collective-permute-start(bf16[1,96,512]{2,1,0:T(8,128)(2,1)S(1)} %collective-permute-done.5), channel_id=1, source_target_pairs={{0,4},{4,8},{8,12},{12,16},{16,20},{20,24},{24,28},{28,0},{1,5},{5... | collective-permute-start | bytes 294920 | tf_op jit(solution)/shard_map/ppermute | solution.py:17
  44.1 12.7 %collective-permute-start.10 = (bf16[8,1,96,512]{3,2,1,0:T(8,128)(2,1)S(1)}, bf16[8,1,96,512]{3,2,1,0:T(8,128)(2,1)}, u32[]{:S(2)}, u32[]{:S(2)}) collective-permute-start(bf16[8,1,96,512]{3,2,1,0:T(8,128)(2,1)S(1)} %bitcast_dynamic-update-slice_fusion), channel_id=1, source_target_pairs={{0,1},{1,2},{2,3},{3,0},{4,5},{5,6},{6,7},{7,4},{8,9},{9,10},{10,1... | collective-permute-start | bytes 2359304 | tf_op jit(solution)/shard_map/ppermute | solution.py:17
  46.0 12.8 %collective-permute-start.11 = (bf16[8,1,96,512]{3,2,1,0:T(8,128)(2,1)S(1)}, bf16[8,1,96,512]{3,2,1,0:T(8,128)(2,1)S(1)}, u32[]{:S(2)}, u32[]{:S(2)}) collective-permute-start(bf16[8,1,96,512]{3,2,1,0:T(8,128)(2,1)S(1)} %bitcast_dynamic-update-slice_fusion), channel_id=1, source_target_pairs={{0,3},{1,0},{2,1},{3,2},{4,7},{5,4},{6,5},{7,6},{8,11},{9,8},{10,9... | collective-permute-start | bytes 2359304 | tf_op jit(solution)/shard_map/ppermute | solution.py:17
  47.9 9.9 %collective-permute-start.15 = (bf16[2,1,96,512]{3,2,1,0:T(8,128)(2,1)}, bf16[2,1,96,512]{3,2,1,0:T(8,128)(2,1)}, u32[]{:S(2)}, u32[]{:S(2)}) collective-permute-start(bf16[2,1,96,512]{3,2,1,0:T(8,128)(2,1)} %get-tuple-element.29), channel_id=1, source_target_pairs={{0,2},{1,3},{2,0},{3,1},{36,38},{37,39},{38,36},{39,37},{72,74},{7... | collective-permute-start | bytes 589832 | tf_op jit(solution)/shard_map/ppermute | solution.py:83
  58.8 16.3 %copy-start.1 = (bf16[8,1,96,512]{3,2,1,0:T(8,128)(2,1)}, bf16[8,1,96,512]{3,2,1,0:T(8,128)(2,1)S(1)}, u32[]{:S(2)}) copy-start(bf16[8,1,96,512]{3,2,1,0:T(8,128)(2,1)S(1)} %collective-permute-done.11) | copy-start | bytes 2359300
  58.9 29.9 %collective-permute-start.20 = (bf16[768,512]{1,0:T(8,128)(2,1)S(1)}, bf16[768,512]{1,0:T(8,128)(2,1)}, u32[]{:S(2)}, u32[]{:S(2)}) collective-permute-start(bf16[768,512]{1,0:T(8,128)(2,1)S(1)} %bitcast.93), channel_id=1, source_target_pairs={{0,224},{1,225},{2,226},{3,227},{36,228},{37,229},{38,230},{39,231... | collective-permute-start | bytes 2359304 | tf_op jit(solution)/shard_map/ppermute | solution.py:83
  60.4 30.0 %collective-permute-start.19 = (bf16[768,512]{1,0:T(8,128)(2,1)S(1)}, bf16[768,512]{1,0:T(8,128)(2,1)}, u32[]{:S(2)}, u32[]{:S(2)}) collective-permute-start(bf16[768,512]{1,0:T(8,128)(2,1)S(1)} %bitcast.94), channel_id=1, source_target_pairs={{0,96},{1,97},{2,98},{3,99},{36,100},{37,101},{38,102},{39,103},{7... | collective-permute-start | bytes 2359304 | tf_op jit(solution)/shard_map/ppermute | solution.py:83
  62.0 33.5 %collective-permute-start.21 = (bf16[768,512]{1,0:T(8,128)(2,1)S(1)}, bf16[768,512]{1,0:T(8,128)(2,1)}, u32[]{:S(2)}, u32[]{:S(2)}) collective-permute-start(bf16[768,512]{1,0:T(8,128)(2,1)S(1)} %bitcast.95), channel_id=1, source_target_pairs={{0,160},{1,161},{2,162},{3,163},{36,164},{37,165},{38,166},{39,167... | collective-permute-start | bytes 2359304 | tf_op jit(solution)/shard_map/ppermute | solution.py:83
  72.7 19.0 %slice-start = ((s8[4718592]{0:T(1024)(128)(4,1)}), s8[4194304]{0:T(1024)(128)(4,1)S(1)}, s32[]{:S(2)}) async-start(s8[4718592]{0:T(1024)(128)(4,1)} %bitcast.107), calls=%async_computation.2 | async-start | bytes 8388608
  72.8 18.9 %slice-start.1 = ((s8[4718592]{0:T(1024)(128)(4,1)}), s8[524288]{0:T(1024)(128)(4,1)S(1)}, s32[]{:S(2)}) async-start(s8[4718592]{0:T(1024)(128)(4,1)} %bitcast.107), calls=%async_computation.3 | async-start | bytes 1048576
  72.8 10.9 %collective-permute-start.13 = (bf16[4,1,96,512]{3,2,1,0:T(8,128)(2,1)S(1)}, bf16[4,1,96,512]{3,2,1,0:T(8,128)(2,1)S(1)}, u32[]{:S(2)}, u32[]{:S(2)}) collective-permute-start(bf16[4,1,96,512]{3,2,1,0:T(8,128)(2,1)S(1)} %slice.19), channel_id=1, source_target_pairs={{0,3},{1,0},{2,1},{3,2},{4,7},{5,4},{6,5},{7,6},{8,11},{9,8},{10,9... | collective-permute-start | bytes 1179656 | tf_op jit(solution)/shard_map/ppermute | solution.py:17
  75.1 10.2 %collective-permute-start.12 = (bf16[4,1,96,512]{3,2,1,0:T(8,128)(2,1)S(1)}, bf16[4,1,96,512]{3,2,1,0:T(8,128)(2,1)S(1)}, u32[]{:S(2)}, u32[]{:S(2)}) collective-permute-start(bf16[4,1,96,512]{3,2,1,0:T(8,128)(2,1)S(1)} %slice.18), channel_id=1, source_target_pairs={{0,1},{1,2},{2,3},{3,0},{4,5},{5,6},{6,7},{7,4},{8,9},{9,10},{10,1... | collective-permute-start | bytes 1179656 | tf_op jit(solution)/shard_map/ppermute | solution.py:17
  81.0 10.6 %copy-start.4 = (bf16[512,768]{1,0:T(8,128)(2,1)}, bf16[512,768]{1,0:T(8,128)(2,1)S(1)}, u32[]{:S(2)}) copy-start(bf16[512,768]{1,0:T(8,128)(2,1)S(1)} %convolution_convert_fusion.1) | copy-start | bytes 2359300
  83.7 19.0 %collective-permute-start.18 = (bf16[768,512]{1,0:T(8,128)(2,1)S(1)}, bf16[768,512]{1,0:T(8,128)(2,1)}, u32[]{:S(2)}, u32[]{:S(2)}) collective-permute-start(bf16[768,512]{1,0:T(8,128)(2,1)S(1)} %get-tuple-element.25), channel_id=1, source_target_pairs={{0,128},{1,129},{2,130},{3,131},{36,132},{37,133},{38,134},{39,135... | collective-permute-start | bytes 2359304 | tf_op jit(solution)/shard_map/ppermute | solution.py:83
  85.3 17.5 %collective-permute-start.17 = (bf16[768,512]{1,0:T(8,128)(2,1)S(1)}, bf16[768,512]{1,0:T(8,128)(2,1)}, u32[]{:S(2)}, u32[]{:S(2)}) collective-permute-start(bf16[768,512]{1,0:T(8,128)(2,1)S(1)} %get-tuple-element.25), channel_id=1, source_target_pairs={{0,192},{1,193},{2,194},{3,195},{36,196},{37,197},{38,198},{39,199... | collective-permute-start | bytes 2359304 | tf_op jit(solution)/shard_map/ppermute | solution.py:83
  87.3 1.4 copy-start.2
  88.8 14.0 %collective-permute-start.16 = (bf16[768,512]{1,0:T(8,128)(2,1)S(1)}, bf16[768,512]{1,0:T(8,128)(2,1)}, u32[]{:S(2)}, u32[]{:S(2)}) collective-permute-start(bf16[768,512]{1,0:T(8,128)(2,1)S(1)} %get-tuple-element.25), channel_id=1, source_target_pairs={{0,64},{1,65},{2,66},{3,67},{36,68},{37,69},{38,70},{39,71},{72,13... | collective-permute-start | bytes 2359304 | tf_op jit(solution)/shard_map/ppermute | solution.py:83
  90.4 12.3 %collective-permute-start.22 = (bf16[768,512]{1,0:T(8,128)(2,1)}, bf16[768,512]{1,0:T(8,128)(2,1)S(1)}, u32[]{:S(2)}, u32[]{:S(2)}) collective-permute-start(bf16[768,512]{1,0:T(8,128)(2,1)} %get-tuple-element.24), channel_id=1, source_target_pairs={{0,32},{1,33},{2,34},{3,35},{36,4},{37,5},{38,6},{39,7},{72,104},{... | collective-permute-start | bytes 2359304 | tf_op jit(solution)/shard_map/ppermute | solution.py:83
  95.5 10.0 %collective-permute-start.14 = (bf16[512,768]{1,0:T(8,128)(2,1)}, bf16[512,768]{1,0:T(8,128)(2,1)}, u32[]{:S(2)}, u32[]{:S(2)}) collective-permute-start(bf16[512,768]{1,0:T(8,128)(2,1)} %get-tuple-element.40), channel_id=1, source_target_pairs={{0,32},{32,0},{1,33},{33,1},{2,34},{34,2},{3,35},{35,3},{4,36},{36... | collective-permute-start | bytes 2359304 | tf_op jit(solution)/shard_map/ppermute | solution.py:92
  102.7 2.8 %copy-start.5 = (bf16[512,768]{1,0:T(8,128)(2,1)S(1)}, bf16[512,768]{1,0:T(8,128)(2,1)}, u32[]{:S(2)}) copy-start(bf16[512,768]{1,0:T(8,128)(2,1)} %copy-done.4) | copy-start | bytes 2359300
  102.7 2.8 %copy-start.6 = (bf16[512,768]{1,0:T(8,128)(2,1)S(1)}, bf16[512,768]{1,0:T(8,128)(2,1)}, u32[]{:S(2)}) copy-start(bf16[512,768]{1,0:T(8,128)(2,1)} %get-tuple-element.41) | copy-start | bytes 2359300
  105.5 3.2 %copy-start.8 = (s32[2,48]{1,0:T(2,128)S(1)}, s32[2,48]{1,0:T(2,128)}, u32[]{:S(2)}) copy-start(s32[2,48]{1,0:T(2,128)} %param.5) | copy-start | bytes 1156
  106.9 52.1 %copy-start.7 = (f32[2,512,64]{1,2,0:T(8,128)S(1)}, f32[2,512,64]{1,2,0:T(8,128)}, u32[]{:S(2)}) copy-start(f32[2,512,64]{1,2,0:T(8,128)} %param.9) | copy-start | bytes 786436
  107.0 6.2 %collective-permute-start.23 = (bf16[128,768]{1,0:T(8,128)(2,1)S(1)}, bf16[128,768]{1,0:T(8,128)(2,1)S(1)}, u32[]{:S(2)}, u32[]{:S(2)}) collective-permute-start(bf16[128,768]{1,0:T(8,128)(2,1)S(1)} %get-tuple-element.26), channel_id=1, source_target_pairs={{0,128},{64,192},{128,0},{192,64},{1,129},{65,193},{129,1},{193,65... | collective-permute-start | bytes 589832 | tf_op jit(solution)/shard_map/ppermute | solution.py:17
  107.1 6.1 %collective-permute-start.25 = (bf16[128,768]{1,0:T(8,128)(2,1)S(1)}, bf16[128,768]{1,0:T(8,128)(2,1)S(1)}, u32[]{:S(2)}, u32[]{:S(2)}) collective-permute-start(bf16[128,768]{1,0:T(8,128)(2,1)S(1)} %get-tuple-element.27), channel_id=1, source_target_pairs={{0,192},{64,0},{128,64},{192,128},{1,193},{65,1},{129,65},{193,129... | collective-permute-start | bytes 589832 | tf_op jit(solution)/shard_map/ppermute | solution.py:17
  107.2 8.0 %collective-permute-start.24 = (bf16[128,768]{1,0:T(8,128)(2,1)S(1)}, bf16[128,768]{1,0:T(8,128)(2,1)S(1)}, u32[]{:S(2)}, u32[]{:S(2)}) collective-permute-start(bf16[128,768]{1,0:T(8,128)(2,1)S(1)} %get-tuple-element.28), channel_id=1, source_target_pairs={{0,64},{64,128},{128,192},{192,0},{1,65},{65,129},{129,193},{193,1... | collective-permute-start | bytes 589832 | tf_op jit(solution)/shard_map/ppermute | solution.py:17
  115.7 3.8 %collective-permute-start.27 = (bf16[32,512]{1,0:T(8,128)(2,1)S(1)}, bf16[32,512]{1,0:T(8,128)(2,1)S(1)}, u32[]{:S(2)}, u32[]{:S(2)}) collective-permute-start(bf16[32,512]{1,0:T(8,128)(2,1)S(1)} %get-tuple-element.37), channel_id=1, source_target_pairs={{0,1},{1,0},{2,3},{3,2},{4,5},{5,4},{6,7},{7,6},{8,9},{9,8},{10,11... | collective-permute-start | bytes 98312 | tf_op jit(solution)/shard_map/ppermute | solution.py:107
  116.6 4.0 %collective-permute-start.29 = (bf16[32,512]{1,0:T(8,128)(2,1)S(1)}, bf16[32,512]{1,0:T(8,128)(2,1)S(1)}, u32[]{:S(2)}, u32[]{:S(2)}) collective-permute-start(bf16[32,512]{1,0:T(8,128)(2,1)S(1)} %get-tuple-element.38), channel_id=1, source_target_pairs={{0,3},{1,2},{2,1},{3,0},{4,7},{5,6},{6,5},{7,4},{8,11},{9,10},{10,... | collective-permute-start | bytes 98312 | tf_op jit(solution)/shard_map/ppermute | solution.py:107
  118.4 4.3 %collective-permute-start.28 = (bf16[32,512]{1,0:T(8,128)(2,1)S(1)}, bf16[32,512]{1,0:T(8,128)(2,1)S(1)}, u32[]{:S(2)}, u32[]{:S(2)}) collective-permute-start(bf16[32,512]{1,0:T(8,128)(2,1)S(1)} %get-tuple-element.39), channel_id=1, source_target_pairs={{0,2},{1,3},{2,0},{3,1},{4,6},{5,7},{6,4},{7,5},{8,10},{9,11},{10,... | collective-permute-start | bytes 98312 | tf_op jit(solution)/shard_map/ppermute | solution.py:107
  123.4 20.8 %all-to-all-start = ((bf16[8,32,512]{2,1,0:T(8,128)(2,1)}), bf16[8,32,512]{2,1,0:T(8,128)(2,1)S(1)}, u32[]{:S(2)}, u32[]{:S(2)}) async-start(bf16[8,32,512]{2,1,0:T(8,128)(2,1)} %broadcast_in_dim.68), calls=%async_computation | async-start | bytes 524288 | tf_op jit(solution)/shard_map/all_to_all | solution.py:119
  134.8 5.0 %collective-permute-start.26 = (bf16[64,768]{1,0:T(8,128)(2,1)S(1)}, bf16[64,768]{1,0:T(8,128)(2,1)S(1)}, u32[]{:S(2)}, u32[]{:S(2)}) collective-permute-start(bf16[64,768]{1,0:T(8,128)(2,1)S(1)} %dynamic-slice_bitcast_fusion.3), channel_id=1, source_target_pairs={{0,32},{32,0},{1,33},{33,1},{2,34},{34,2},{3,35},{35,3},{4,36},{36... | collective-permute-start | bytes 294920 | tf_op jit(solution)/shard_map/ppermute | solution.py:133
  144.2 5.3 %collective-permute-start.32 = (bf16[32,512]{1,0:T(8,128)(2,1)S(1)}, bf16[32,512]{1,0:T(8,128)(2,1)S(1)}, u32[]{:S(2)}, u32[]{:S(2)}) collective-permute-start(bf16[32,512]{1,0:T(8,128)(2,1)S(1)} %reduce_sum.12), channel_id=1, source_target_pairs={{0,3},{1,2},{2,1},{3,0},{4,7},{5,6},{6,5},{7,4},{8,11},{9,10},{10,... | collective-permute-start | bytes 98312 | tf_op jit(solution)/shard_map/ppermute | solution.py:107
  144.5 5.0 %collective-permute-start.31 = (bf16[32,512]{1,0:T(8,128)(2,1)S(1)}, bf16[32,512]{1,0:T(8,128)(2,1)S(1)}, u32[]{:S(2)}, u32[]{:S(2)}) collective-permute-start(bf16[32,512]{1,0:T(8,128)(2,1)S(1)} %reduce_sum.12), channel_id=1, source_target_pairs={{0,2},{1,3},{2,0},{3,1},{4,6},{5,7},{6,4},{7,5},{8,10},{9,11},{10,... | collective-permute-start | bytes 98312 | tf_op jit(solution)/shard_map/ppermute | solution.py:107
  146.7 2.8 %collective-permute-start.30 = (bf16[32,512]{1,0:T(8,128)(2,1)S(1)}, bf16[32,512]{1,0:T(8,128)(2,1)S(1)}, u32[]{:S(2)}, u32[]{:S(2)}) collective-permute-start(bf16[32,512]{1,0:T(8,128)(2,1)S(1)} %reduce_sum.12), channel_id=1, source_target_pairs={{0,1},{1,0},{2,3},{3,2},{4,5},{5,4},{6,7},{7,6},{8,9},{9,8},{10,11... | collective-permute-start | bytes 98312 | tf_op jit(solution)/shard_map/ppermute | solution.py:107
  149.6 9.4 %collective-permute-start.33 = (bf16[64,512]{1,0:T(8,128)(2,1)S(1)}, bf16[64,512]{1,0:T(8,128)(2,1)S(1)}, u32[]{:S(2)}, u32[]{:S(2)}) collective-permute-start(bf16[64,512]{1,0:T(8,128)(2,1)S(1)} %dynamic-slice_bitcast_fusion.4), channel_id=1, source_target_pairs={{0,32},{32,0},{1,33},{33,1},{2,34},{34,2},{3,35},{35,3},{4,36},{36... | collective-permute-start | bytes 196616 | tf_op jit(solution)/shard_map/ppermute | solution.py:133
Sparse Core Ops, SparseCore 0:
  21.1 50.5 all-gather.1
where the time goes:
time: 167 us
  starting transfers between devices  73.3 us (44%)
  waiting for transfers between devices  50 us (30%)
  between operations  14.8 us (9%)
  matrix products  11.2 us (7%)
  other arithmetic  9.54 us (6%)
  local copies, waits for them, and re-layouts  7.73 us (5%)
    ppermute x17, waiting for transfers between devices, shift(): lax.ppermute(array, axis, [(i, (i + by) % size) for i in range(size)])  31.2 us
    ppermute x17, starting transfers between devices, shift(): lax.ppermute(array, axis, [(i, (i + by) % size) for i in range(size)])  22.9 us
    ppermute x2, starting transfers between devices, own_slab_of_both(): got = lax.ppermute(given, 'core', [(0, 1), (1, 0)])  12.6 us
    ppermute x8, starting transfers between devices, from_root(): return lax.ppermute(array, ALL, pairs)  12.1 us
    all_to_all x1, starting transfers between devices, summed_over_col(): part = lax.all_to_all(copies, 'z', split_axis=0, concat_axis=0, tiled=True)  11.4 us
    dot_general x2, matrix products, partial_of(): jnp.einsum('qj,pq->jp', panel, inverse_block, preferred_element_type=F32)  9.75 us
    all_gather x1, waiting for transfers between devices, panel_y_then_z(): return lax.all_gather(part, 'z', axis=0, tiled=True)  8.13 us
    ppermute x1, starting transfers between devices, pair_sum(): lax.ppermute(jnp.where(first, partial[1], partial[0]), 'core', [(0, 1), (...  7.18 us
  transfers between devices with their start and end apart: 36, of which 16 were waited for; matrix products, arithmetic and copies ran while one was open for 13% of the time, Pallas kernels for 0%

commit v1 on v0

--- a/solution.py
+++ b/solution.py
@@ -51,8 +51,18 @@
 
 
 def panel_y_then_z(piece):
+
+    def _serve_lane(load):
+        u1 = lax.all_to_all(
+            jnp.stack([load for _ in range(lax.axis_size("z"))]),
+            axis_name="z",
+            split_axis=0,
+            concat_axis=0,
+        )
+        return jnp.concatenate(u1, axis=0)
+
     part = placed_by_owner(direct_ring(piece, "y", YS), lax.axis_index("y"), 0)
-    return lax.all_gather(part, "z", axis=0, tiled=True)
+    return _serve_lane(part)
 
 
 def near_z_then_y(piece):

time: 167 us -> 223 us (1.34)
  waiting for transfers between devices: 50 us -> 98.4 us
  starting transfers between devices: 73.3 us -> 92.7 us
  between operations: 14.8 us -> 1.42 us
    ppermute x17, waiting for transfers between devices: 31.2 us -> 89 us  [shift(): lax.ppermute(array, axis, [(i, (i + by) % size) for i in range(size)])]
    all_gather x1 -> x0, waiting for transfers between devices: 8.13 us -> none  [panel_y_then_z(): return lax.all_gather(part, 'z', axis=0, tiled=True)]
    ppermute x1, starting transfers between devices: 7.18 us -> 14.5 us  [pair_sum(): lax.ppermute(jnp.where(first, partial[1], partial[0]), 'core', [(0, 1), (...]
    all_to_all x0 -> x1, starting transfers between devices: none -> 6.38 us  [_serve_lane(): lax.all_to_all(jnp.stack([load for _ in range(lax.axis_size('z'))]), axis...]
    ppermute x17, starting transfers between devices: 22.9 us -> 27.8 us  [shift(): lax.ppermute(array, axis, [(i, (i + by) % size) for i in range(size)])]
  transfers between devices with their start and end apart: 36 -> 36, of which waited for: 16 -> 14; matrix products, arithmetic and copies ran while one was open for 13% -> 10% of each run, Pallas kernels for 0% -> 0%
where the time goes in v1:
time: 223 us; the launch traced here: 222 us
  waiting for transfers between devices  98.4 us (44%)
  starting transfers between devices  92.7 us (42%)
  matrix products  11.3 us (5%)
  other arithmetic  9.49 us (4%)
  local copies, waits for them, and re-layouts  9 us (4%)
    ppermute x17, waiting for transfers between devices, shift(): lax.ppermute(array, axis, [(i, (i + by) % size) for i in range(size)])  89 us
    ppermute x17, starting transfers between devices, shift(): lax.ppermute(array, axis, [(i, (i + by) % size) for i in range(size)])  27.8 us
    ppermute x2, starting transfers between devices, own_slab_of_both(): got = lax.ppermute(given, 'core', [(0, 1), (1, 0)])  14.6 us
    ppermute x1, starting transfers between devices, pair_sum(): lax.ppermute(jnp.where(first, partial[1], partial[0]), 'core', [(0, 1), (...  14.5 us
    ppermute x8, starting transfers between devices, from_root(): return lax.ppermute(array, ALL, pairs)  12.1 us
    dot_general x2, matrix products, partial_of(): jnp.einsum('qj,pq->jp', panel, inverse_block, preferred_element_type=F32)  9.79 us
    all_to_all x1, starting transfers between devices, summed_over_col(): part = lax.all_to_all(copies, 'z', split_axis=0, concat_axis=0, tiled=True)  9.77 us
    ppermute x6, starting transfers between devices, exchanged(): return lax.ppermute(array, axis, [(i, i ^ by) for i in range(size)])  7.57 us
  transfers between devices with their start and end apart: 36, of which 14 were waited for; matrix products, arithmetic and copies ran while one was open for 10% of the time, Pallas kernels for 0%

profile of v1, /device:TPU:1, one launch (start us, length us, event | category | flops | bytes accessed | tf_op | source)
XLA Modules:
  0.0 222.3 jit_solution(16417040624497888058)
XLA Ops:
  1.9 1.2 fusion
  3.1 3.8 %collective-permute-start.1 = (bf16[96,512]{1,0:T(8,128)(2,1)S(1)}, bf16[96,512]{1,0:T(8,128)(2,1)S(1)}, u32[]{:S(2)}, u32[]{:S(2)}) collective-permute-start(bf16[96,512]{1,0:T(8,128)(2,1)S(1)} %get-tuple-element.36), channel_id=1, source_target_pairs={{0,2},{1,3},{2,0},{3,1},{4,6},{5,7},{6,4},{7,5},{8,10},{9,11},{10,... | collective-permute-start | bytes 294920 | tf_op jit(solution)/shard_map/ppermute | solution.py:17
  7.4 2.3 %collective-permute-start.2 = (bf16[96,512]{1,0:T(8,128)(2,1)S(1)}, bf16[96,512]{1,0:T(8,128)(2,1)S(1)}, u32[]{:S(2)}, u32[]{:S(2)}) collective-permute-start(bf16[96,512]{1,0:T(8,128)(2,1)S(1)} %get-tuple-element.36), channel_id=1, source_target_pairs={{0,3},{1,0},{2,1},{3,2},{4,7},{5,4},{6,5},{7,6},{8,11},{9,8},{10,9... | collective-permute-start | bytes 294920 | tf_op jit(solution)/shard_map/ppermute | solution.py:17
  9.8 3.8 %collective-permute-done = bf16[96,512]{1,0:T(8,128)(2,1)S(1)} collective-permute-done((bf16[96,512]{1,0:T(8,128)(2,1)S(1)}, bf16[96,512]{1,0:T(8,128)(2,1)S(1)}, u32[]{:S(2)}, u32[]{:S(2)}) %collective-permute-start) | collective-permute-done | bytes 98336 | tf_op jit(solution)/shard_map/ppermute | solution.py:17
  13.7 2.0 stack.14
  15.6 6.4 %all-to-all-start = ((bf16[8,384,512]{2,1,0:T(8,128)(2,1)}), bf16[8,384,512]{2,1,0:T(8,128)(2,1)}, u32[]{:S(2)}, u32[]{:S(2)}) async-start(bf16[8,384,512]{2,1,0:T(8,128)(2,1)} %stack.14), calls=%async_computation | async-start | bytes 6291456 | tf_op jit(solution)/shard_map/all_to_all | solution.py:56
  22.0 1.5 collective-permute-start.3
  23.5 1.2 collective-permute-start.7
  25.0 60.5 %collective-permute-done.3 = bf16[1,96,512]{2,1,0:T(8,128)(2,1)S(1)} collective-permute-done((bf16[1,96,512]{2,1,0:T(8,128)(2,1)S(1)}, bf16[1,96,512]{2,1,0:T(8,128)(2,1)S(1)}, u32[]{:S(2)}, u32[]{:S(2)}) %collective-permute-start.3) | collective-permute-done | bytes 98336 | tf_op jit(solution)/shard_map/ppermute | solution.py:17
  85.5 6.4 %collective-permute-start.4 = (bf16[1,96,512]{2,1,0:T(8,128)(2,1)S(1)}, bf16[1,96,512]{2,1,0:T(8,128)(2,1)S(1)}, u32[]{:S(2)}, u32[]{:S(2)}) collective-permute-start(bf16[1,96,512]{2,1,0:T(8,128)(2,1)S(1)} %collective-permute-done.3), channel_id=1, source_target_pairs={{0,4},{4,8},{8,12},{12,16},{16,20},{20,24},{24,28},{28,0},{1,5},{5... | collective-permute-start | bytes 294920 | tf_op jit(solution)/shard_map/ppermute | solution.py:17
  91.9 2.9 %collective-permute-start.8 = (bf16[1,96,512]{2,1,0:T(8,128)(2,1)S(1)}, bf16[1,96,512]{2,1,0:T(8,128)(2,1)S(1)}, u32[]{:S(2)}, u32[]{:S(2)}) collective-permute-start(bf16[1,96,512]{2,1,0:T(8,128)(2,1)S(1)} %collective-permute-done.7), channel_id=1, source_target_pairs={{0,28},{4,0},{8,4},{12,8},{16,12},{20,16},{24,20},{28,24},{1,29},{... | collective-permute-start | bytes 294920 | tf_op jit(solution)/shard_map/ppermute | solution.py:17
  94.8 2.1 collective-permute-done.4
  96.9 2.7 %collective-permute-start.9 = (bf16[1,96,512]{2,1,0:T(8,128)(2,1)S(1)}, bf16[1,96,512]{2,1,0:T(8,128)(2,1)S(1)}, u32[]{:S(2)}, u32[]{:S(2)}) collective-permute-start(bf16[1,96,512]{2,1,0:T(8,128)(2,1)S(1)} %collective-permute-done.8), channel_id=1, source_target_pairs={{0,28},{4,0},{8,4},{12,8},{16,12},{20,16},{24,20},{28,24},{1,29},{... | collective-permute-start | bytes 294920 | tf_op jit(solution)/shard_map/ppermute | solution.py:17
  99.6 2.0 collective-permute-done.5
  101.6 5.5 %collective-permute-done.6 = bf16[1,96,512]{2,1,0:T(8,128)(2,1)S(1)} collective-permute-done((bf16[1,96,512]{2,1,0:T(8,128)(2,1)S(1)}, bf16[1,96,512]{2,1,0:T(8,128)(2,1)S(1)}, u32[]{:S(2)}, u32[]{:S(2)}) %collective-permute-start.6) | collective-permute-done | bytes 98336 | tf_op jit(solution)/shard_map/ppermute | solution.py:17
  107.1 2.5 %collective-permute-start.10 = (bf16[8,1,96,512]{3,2,1,0:T(8,128)(2,1)S(1)}, bf16[8,1,96,512]{3,2,1,0:T(8,128)(2,1)}, u32[]{:S(2)}, u32[]{:S(2)}) collective-permute-start(bf16[8,1,96,512]{3,2,1,0:T(8,128)(2,1)S(1)} %bitcast_dynamic-update-slice_fusion), channel_id=1, source_target_pairs={{0,1},{1,2},{2,3},{3,0},{4,5},{5,6},{6,7},{7,4},{8,9},{9,10},{10,1... | collective-permute-start | bytes 2359304 | tf_op jit(solution)/shard_map/ppermute | solution.py:17
  110.8 1.3 collective-permute-start.15
  112.1 8.7 %collective-permute-done.10 = bf16[8,1,96,512]{3,2,1,0:T(8,128)(2,1)} collective-permute-done((bf16[8,1,96,512]{3,2,1,0:T(8,128)(2,1)S(1)}, bf16[8,1,96,512]{3,2,1,0:T(8,128)(2,1)}, u32[]{:S(2)}, u32[]{:S(2)}) %collective-permute-start.10) | collective-permute-done | bytes 786464 | tf_op jit(solution)/shard_map/ppermute | solution.py:17
  121.8 0.9 constant_dynamic-update-slice_fusion
  122.8 1.6 collective-permute-start.20
  124.4 1.6 collective-permute-start.19
  126.0 1.5 collective-permute-start.21
  127.5 1.0 slice.18
  128.6 1.3 collective-permute-start.13
  130.7 5.9 %convolution_convert_fusion.1 = bf16[512,768]{1,0:T(8,128)(2,1)S(1)} fusion(bf16[3072,512]{1,0:T(8,128)(2,1)} %bitcast.1, bf16[768,3072]{1,0:T(8,128)(2,1)} %param.8), kind=kOutput, calls=%fused_computation.2 | convolution fusion | flops 2416312320 | bytes 8650752 | tf_op jit(solution)/shard_map/qj,pq->jp/dot_general | solution.py:164
  136.7 2.6 %broadcast_select_fusion = (bf16[768,512]{1,0:T(8,128)(2,1)}, bf16[768,512]{1,0:T(8,128)(2,1)S(1)}) fusion(pred[]{:T(512)S(6)} %eq.63, bf16[2,4,96,512]{3,2,1,0:T(8,128)(2,1)S(1)} %dynamic-slice_dynamic-update-slice_fusion, bf16[3072,512]{1,0:T(8,128)(2,1)} %bitcast.1, s32[]{:T(128)S(6)} %select_n.299), kind=kLoop, calls=%fused_computation.9 | loop fusion | flops 393216 | bytes 3145733 | tf_op jit(solution)/shard_map/jit(_where)/select_n | solution.py:183
  139.3 1.6 collective-permute-start.18
  140.8 1.6 collective-permute-start.17
  142.9 1.3 constant_dynamic-update-slice_fusion.3
  144.3 1.6 collective-permute-start.16
  145.9 1.3 collective-permute-start.22
  147.2 3.8 %broadcast_select_fusion.1 = (bf16[512,768]{1,0:T(8,128)(2,1)}, bf16[512,768]{1,0:T(8,128)(2,1)}) fusion(bf16[512,768]{1,0:T(8,128)(2,1)S(1)} %convolution_convert_fusion.1, pred[]{:T(512)S(6)} %eq.63, bf16[3072,512]{1,0:T(8,128)(2,1)S(1)} %bitcast.97, bf16[768,3072]{1,0:T(8,128)(2,1)S(1)} %bitcast.109), kind=kOutput, calls=%fused_computation.10 | convolution fusion | flops 2416705536 | bytes 10223617 | tf_op jit(solution)/shard_map/qj,pq->jp/dot_general | solution.py:164
  151.1 14.5 %collective-permute-start.14 = (bf16[512,768]{1,0:T(8,128)(2,1)}, bf16[512,768]{1,0:T(8,128)(2,1)}, u32[]{:S(2)}, u32[]{:S(2)}) collective-permute-start(bf16[512,768]{1,0:T(8,128)(2,1)} %get-tuple-element.40), channel_id=1, source_target_pairs={{0,32},{32,0},{1,33},{33,1},{2,34},{34,2},{3,35},{35,3},{4,36},{36... | collective-permute-start | bytes 2359304 | tf_op jit(solution)/shard_map/ppermute | solution.py:102
  165.6 2.7 %add_select_fusion = bf16[768,512]{1,0:T(8,128)(2,1)S(1)} fusion(bf16[768,512]{1,0:T(8,128)(2,1)S(1)} %collective-permute-done.22, bf16[768,512]{1,0:T(8,128)(2,1)} %collective-permute-done.21, bf16[768,512]{1,0:T(8,128)(2,1)} %collective-permute-done.19, bf16[768,512]{1,0:T(8,128)(2,1)} %collective-permute-done.20, ...), kind=kLoop, calls=%fused_computation.8 | loop fusion | flops 3145728 | bytes 7864322 | tf_op jit(solution)/shard_map/jit(_where)/select_n | solution.py:186
  168.4 1.4 add_convert_fusion
  170.1 1.5 collective-permute-start.24
  171.7 4.4 %collective-permute-done.23 = bf16[128,768]{1,0:T(8,128)(2,1)S(1)} collective-permute-done((bf16[128,768]{1,0:T(8,128)(2,1)S(1)}, bf16[128,768]{1,0:T(8,128)(2,1)S(1)}, u32[]{:S(2)}, u32[]{:S(2)}) %collective-permute-start.23) | collective-permute-done | bytes 196640 | tf_op jit(solution)/shard_map/ppermute | solution.py:17
  176.1 2.0 collective-permute-done.24
  178.9 2.9 %collective-permute-start.29 = (bf16[32,512]{1,0:T(8,128)(2,1)S(1)}, bf16[32,512]{1,0:T(8,128)(2,1)S(1)}, u32[]{:S(2)}, u32[]{:S(2)}) collective-permute-start(bf16[32,512]{1,0:T(8,128)(2,1)S(1)} %get-tuple-element.38), channel_id=1, source_target_pairs={{0,3},{1,2},{2,1},{3,0},{4,7},{5,6},{6,5},{7,4},{8,11},{9,10},{10,... | collective-permute-start | bytes 98312 | tf_op jit(solution)/shard_map/ppermute | solution.py:117
  181.7 1.1 collective-permute-start.28
  183.0 3.0 %collective-permute-done.28 = bf16[32,512]{1,0:T(8,128)(2,1)S(1)} collective-permute-done((bf16[32,512]{1,0:T(8,128)(2,1)S(1)}, bf16[32,512]{1,0:T(8,128)(2,1)S(1)}, u32[]{:S(2)}, u32[]{:S(2)}) %collective-permute-start.28) | collective-permute-done | bytes 32800 | tf_op jit(solution)/shard_map/ppermute | solution.py:117
  186.7 9.8 %all-to-all-start.1 = ((bf16[8,32,512]{2,1,0:T(8,128)(2,1)}), bf16[8,32,512]{2,1,0:T(8,128)(2,1)S(1)}, u32[]{:S(2)}, u32[]{:S(2)}) async-start(bf16[8,32,512]{2,1,0:T(8,128)(2,1)} %broadcast_in_dim.65), calls=%async_computation.1 | async-start | bytes 524288 | tf_op jit(solution)/shard_map/all_to_all | solution.py:129
  196.5 5.6 %collective-permute-start.26 = (bf16[64,768]{1,0:T(8,128)(2,1)S(1)}, bf16[64,768]{1,0:T(8,128)(2,1)S(1)}, u32[]{:S(2)}, u32[]{:S(2)}) collective-permute-start(bf16[64,768]{1,0:T(8,128)(2,1)S(1)} %dynamic-slice_bitcast_fusion.3), channel_id=1, source_target_pairs={{0,32},{32,0},{1,33},{33,1},{2,34},{34,2},{3,35},{35,3},{4,36},{36... | collective-permute-start | bytes 294920 | tf_op jit(solution)/shard_map/ppermute | solution.py:143
  202.2 0.9 collective-permute-done.26
  203.1 2.7 %all-to-all-done.1 = bf16[8,32,512]{2,1,0:T(8,128)(2,1)S(1)} async-done(((bf16[8,32,512]{2,1,0:T(8,128)(2,1)}), bf16[8,32,512]{2,1,0:T(8,128)(2,1)S(1)}, u32[]{:S(2)}, u32[]{:S(2)}) %all-to-all-start.1) | async-done | bytes 262176 | tf_op jit(solution)/shard_map/all_to_all | solution.py:129
  206.5 2.0 collective-permute-start.31
  209.3 2.3 %collective-permute-done.30 = bf16[32,512]{1,0:T(8,128)(2,1)S(1)} collective-permute-done((bf16[32,512]{1,0:T(8,128)(2,1)S(1)}, bf16[32,512]{1,0:T(8,128)(2,1)S(1)}, u32[]{:S(2)}, u32[]{:S(2)}) %collective-permute-start.30) | collective-permute-done | bytes 32800 | tf_op jit(solution)/shard_map/ppermute | solution.py:117
  211.6 9.0 %collective-permute-start.33 = (bf16[64,512]{1,0:T(8,128)(2,1)S(1)}, bf16[64,512]{1,0:T(8,128)(2,1)S(1)}, u32[]{:S(2)}, u32[]{:S(2)}) collective-permute-start(bf16[64,512]{1,0:T(8,128)(2,1)S(1)} %dynamic-slice_bitcast_fusion.4), channel_id=1, source_target_pairs={{0,32},{32,0},{1,33},{33,1},{2,34},{34,2},{3,35},{35,3},{4,36},{36... | collective-permute-start | bytes 196616 | tf_op jit(solution)/shard_map/ppermute | solution.py:143
  (104 shorter events, 10.7 us)
Async XLA Ops:
  0.6 1.2 copy-start
  3.1 10.5 %collective-permute-start.1 = (bf16[96,512]{1,0:T(8,128)(2,1)S(1)}, bf16[96,512]{1,0:T(8,128)(2,1)S(1)}, u32[]{:S(2)}, u32[]{:S(2)}) collective-permute-start(bf16[96,512]{1,0:T(8,128)(2,1)S(1)} %get-tuple-element.36), channel_id=1, source_target_pairs={{0,2},{1,3},{2,0},{3,1},{4,6},{5,7},{6,4},{7,5},{8,10},{9,11},{10,... | collective-permute-start | bytes 294920 | tf_op jit(solution)/shard_map/ppermute | solution.py:17
  7.0 6.6 %collective-permute-start = (bf16[96,512]{1,0:T(8,128)(2,1)S(1)}, bf16[96,512]{1,0:T(8,128)(2,1)S(1)}, u32[]{:S(2)}, u32[]{:S(2)}) collective-permute-start(bf16[96,512]{1,0:T(8,128)(2,1)S(1)} %get-tuple-element.36), channel_id=1, source_target_pairs={{0,1},{1,2},{2,3},{3,0},{4,5},{5,6},{6,7},{7,4},{8,9},{9,10},{10,1... | collective-permute-start | bytes 294920 | tf_op jit(solution)/shard_map/ppermute | solution.py:17
  7.4 6.3 %collective-permute-start.2 = (bf16[96,512]{1,0:T(8,128)(2,1)S(1)}, bf16[96,512]{1,0:T(8,128)(2,1)S(1)}, u32[]{:S(2)}, u32[]{:S(2)}) collective-permute-start(bf16[96,512]{1,0:T(8,128)(2,1)S(1)} %get-tuple-element.36), channel_id=1, source_target_pairs={{0,3},{1,0},{2,1},{3,2},{4,7},{5,4},{6,5},{7,6},{8,11},{9,8},{10,9... | collective-permute-start | bytes 294920 | tf_op jit(solution)/shard_map/ppermute | solution.py:17
  15.6 111.9 %all-to-all-start = ((bf16[8,384,512]{2,1,0:T(8,128)(2,1)}), bf16[8,384,512]{2,1,0:T(8,128)(2,1)}, u32[]{:S(2)}, u32[]{:S(2)}) async-start(bf16[8,384,512]{2,1,0:T(8,128)(2,1)} %stack.14), calls=%async_computation | async-start | bytes 6291456 | tf_op jit(solution)/shard_map/all_to_all | solution.py:56
  22.0 63.5 %collective-permute-start.3 = (bf16[1,96,512]{2,1,0:T(8,128)(2,1)S(1)}, bf16[1,96,512]{2,1,0:T(8,128)(2,1)S(1)}, u32[]{:S(2)}, u32[]{:S(2)}) collective-permute-start(bf16[1,96,512]{2,1,0:T(8,128)(2,1)S(1)} %get-tuple-element.35), channel_id=1, source_target_pairs={{0,4},{4,8},{8,12},{12,16},{16,20},{20,24},{24,28},{28,0},{1,5},{5... | collective-permute-start | bytes 294920 | tf_op jit(solution)/shard_map/ppermute | solution.py:17
  23.5 68.4 %collective-permute-start.7 = (bf16[1,96,512]{2,1,0:T(8,128)(2,1)S(1)}, bf16[1,96,512]{2,1,0:T(8,128)(2,1)S(1)}, u32[]{:S(2)}, u32[]{:S(2)}) collective-permute-start(bf16[1,96,512]{2,1,0:T(8,128)(2,1)S(1)} %get-tuple-element.35), channel_id=1, source_target_pairs={{0,28},{4,0},{8,4},{12,8},{16,12},{20,16},{24,20},{28,24},{1,29},{... | collective-permute-start | bytes 294920 | tf_op jit(solution)/shard_map/ppermute | solution.py:17
  85.5 11.4 %collective-permute-start.4 = (bf16[1,96,512]{2,1,0:T(8,128)(2,1)S(1)}, bf16[1,96,512]{2,1,0:T(8,128)(2,1)S(1)}, u32[]{:S(2)}, u32[]{:S(2)}) collective-permute-start(bf16[1,96,512]{2,1,0:T(8,128)(2,1)S(1)} %collective-permute-done.3), channel_id=1, source_target_pairs={{0,4},{4,8},{8,12},{12,16},{16,20},{20,24},{24,28},{28,0},{1,5},{5... | collective-permute-start | bytes 294920 | tf_op jit(solution)/shard_map/ppermute | solution.py:17
  91.9 5.0 %collective-permute-start.8 = (bf16[1,96,512]{2,1,0:T(8,128)(2,1)S(1)}, bf16[1,96,512]{2,1,0:T(8,128)(2,1)S(1)}, u32[]{:S(2)}, u32[]{:S(2)}) collective-permute-start(bf16[1,96,512]{2,1,0:T(8,128)(2,1)S(1)} %collective-permute-done.7), channel_id=1, source_target_pairs={{0,28},{4,0},{8,4},{12,8},{16,12},{20,16},{24,20},{28,24},{1,29},{... | collective-permute-start | bytes 294920 | tf_op jit(solution)/shard_map/ppermute | solution.py:17
  96.9 4.7 %collective-permute-start.5 = (bf16[1,96,512]{2,1,0:T(8,128)(2,1)S(1)}, bf16[1,96,512]{2,1,0:T(8,128)(2,1)S(1)}, u32[]{:S(2)}, u32[]{:S(2)}) collective-permute-start(bf16[1,96,512]{2,1,0:T(8,128)(2,1)S(1)} %collective-permute-done.4), channel_id=1, source_target_pairs={{0,4},{4,8},{8,12},{12,16},{16,20},{20,24},{24,28},{28,0},{1,5},{5... | collective-permute-start | bytes 294920 | tf_op jit(solution)/shard_map/ppermute | solution.py:17
  96.9 10.2 %collective-permute-start.9 = (bf16[1,96,512]{2,1,0:T(8,128)(2,1)S(1)}, bf16[1,96,512]{2,1,0:T(8,128)(2,1)S(1)}, u32[]{:S(2)}, u32[]{:S(2)}) collective-permute-start(bf16[1,96,512]{2,1,0:T(8,128)(2,1)S(1)} %collective-permute-done.8), channel_id=1, source_target_pairs={{0,28},{4,0},{8,4},{12,8},{16,12},{20,16},{24,20},{28,24},{1,29},{... | collective-permute-start | bytes 294920 | tf_op jit(solution)/shard_map/ppermute | solution.py:17
  101.6 5.5 %collective-permute-start.6 = (bf16[1,96,512]{2,1,0:T(8,128)(2,1)S(1)}, bf16[1,96,512]{2,1,0:T(8,128)(2,1)S(1)}, u32[]{:S(2)}, u32[]{:S(2)}) collective-permute-start(bf16[1,96,512]{2,1,0:T(8,128)(2,1)S(1)} %collective-permute-done.5), channel_id=1, source_target_pairs={{0,4},{4,8},{8,12},{12,16},{16,20},{20,24},{24,28},{28,0},{1,5},{5... | collective-permute-start | bytes 294920 | tf_op jit(solution)/shard_map/ppermute | solution.py:17
  107.1 13.7 %collective-permute-start.10 = (bf16[8,1,96,512]{3,2,1,0:T(8,128)(2,1)S(1)}, bf16[8,1,96,512]{3,2,1,0:T(8,128)(2,1)}, u32[]{:S(2)}, u32[]{:S(2)}) collective-permute-start(bf16[8,1,96,512]{3,2,1,0:T(8,128)(2,1)S(1)} %bitcast_dynamic-update-slice_fusion), channel_id=1, source_target_pairs={{0,1},{1,2},{2,3},{3,0},{4,5},{5,6},{6,7},{7,4},{8,9},{9,10},{10,1... | collective-permute-start | bytes 2359304 | tf_op jit(solution)/shard_map/ppermute | solution.py:17
  109.6 13.1 %collective-permute-start.11 = (bf16[8,1,96,512]{3,2,1,0:T(8,128)(2,1)S(1)}, bf16[8,1,96,512]{3,2,1,0:T(8,128)(2,1)S(1)}, u32[]{:S(2)}, u32[]{:S(2)}) collective-permute-start(bf16[8,1,96,512]{3,2,1,0:T(8,128)(2,1)S(1)} %bitcast_dynamic-update-slice_fusion), channel_id=1, source_target_pairs={{0,3},{1,0},{2,1},{3,2},{4,7},{5,4},{6,5},{7,6},{8,11},{9,8},{10,9... | collective-permute-start | bytes 2359304 | tf_op jit(solution)/shard_map/ppermute | solution.py:17
  110.8 11.0 %collective-permute-start.15 = (bf16[2,1,96,512]{3,2,1,0:T(8,128)(2,1)}, bf16[2,1,96,512]{3,2,1,0:T(8,128)(2,1)}, u32[]{:S(2)}, u32[]{:S(2)}) collective-permute-start(bf16[2,1,96,512]{3,2,1,0:T(8,128)(2,1)} %get-tuple-element.29), channel_id=1, source_target_pairs={{0,2},{1,3},{2,0},{3,1},{36,38},{37,39},{38,36},{39,37},{72,74},{7... | collective-permute-start | bytes 589832 | tf_op jit(solution)/shard_map/ppermute | solution.py:93
  122.7 8.0 %copy-start.1 = (bf16[8,1,96,512]{3,2,1,0:T(8,128)(2,1)}, bf16[8,1,96,512]{3,2,1,0:T(8,128)(2,1)S(1)}, u32[]{:S(2)}) copy-start(bf16[8,1,96,512]{3,2,1,0:T(8,128)(2,1)S(1)} %collective-permute-done.11) | copy-start | bytes 2359300
  122.8 21.6 %collective-permute-start.20 = (bf16[768,512]{1,0:T(8,128)(2,1)S(1)}, bf16[768,512]{1,0:T(8,128)(2,1)}, u32[]{:S(2)}, u32[]{:S(2)}) collective-permute-start(bf16[768,512]{1,0:T(8,128)(2,1)S(1)} %bitcast.94), channel_id=1, source_target_pairs={{0,224},{1,225},{2,226},{3,227},{36,228},{37,229},{38,230},{39,231... | collective-permute-start | bytes 2359304 | tf_op jit(solution)/shard_map/ppermute | solution.py:93
  124.4 21.5 %collective-permute-start.19 = (bf16[768,512]{1,0:T(8,128)(2,1)S(1)}, bf16[768,512]{1,0:T(8,128)(2,1)}, u32[]{:S(2)}, u32[]{:S(2)}) collective-permute-start(bf16[768,512]{1,0:T(8,128)(2,1)S(1)} %bitcast.95), channel_id=1, source_target_pairs={{0,96},{1,97},{2,98},{3,99},{36,100},{37,101},{38,102},{39,103},{7... | collective-permute-start | bytes 2359304 | tf_op jit(solution)/shard_map/ppermute | solution.py:93
  126.0 25.1 %collective-permute-start.21 = (bf16[768,512]{1,0:T(8,128)(2,1)S(1)}, bf16[768,512]{1,0:T(8,128)(2,1)}, u32[]{:S(2)}, u32[]{:S(2)}) collective-permute-start(bf16[768,512]{1,0:T(8,128)(2,1)S(1)} %bitcast.96), channel_id=1, source_target_pairs={{0,160},{1,161},{2,162},{3,163},{36,164},{37,165},{38,166},{39,167... | collective-permute-start | bytes 2359304 | tf_op jit(solution)/shard_map/ppermute | solution.py:93
  128.6 18.7 %slice-start = ((s8[4718592]{0:T(1024)(128)(4,1)}), s8[4194304]{0:T(1024)(128)(4,1)S(1)}, s32[]{:S(2)}) async-start(s8[4718592]{0:T(1024)(128)(4,1)} %bitcast.108), calls=%async_computation.2 | async-start | bytes 8388608
  128.6 18.6 %slice-start.1 = ((s8[4718592]{0:T(1024)(128)(4,1)}), s8[524288]{0:T(1024)(128)(4,1)S(1)}, s32[]{:S(2)}) async-start(s8[4718592]{0:T(1024)(128)(4,1)} %bitcast.108), calls=%async_computation.3 | async-start | bytes 1048576
  128.6 10.7 %collective-permute-start.13 = (bf16[4,1,96,512]{3,2,1,0:T(8,128)(2,1)S(1)}, bf16[4,1,96,512]{3,2,1,0:T(8,128)(2,1)S(1)}, u32[]{:S(2)}, u32[]{:S(2)}) collective-permute-start(bf16[4,1,96,512]{3,2,1,0:T(8,128)(2,1)S(1)} %slice.19), channel_id=1, source_target_pairs={{0,3},{1,0},{2,1},{3,2},{4,7},{5,4},{6,5},{7,6},{8,11},{9,8},{10,9... | collective-permute-start | bytes 1179656 | tf_op jit(solution)/shard_map/ppermute | solution.py:17
  129.9 11.0 %collective-permute-start.12 = (bf16[4,1,96,512]{3,2,1,0:T(8,128)(2,1)S(1)}, bf16[4,1,96,512]{3,2,1,0:T(8,128)(2,1)S(1)}, u32[]{:S(2)}, u32[]{:S(2)}) collective-permute-start(bf16[4,1,96,512]{3,2,1,0:T(8,128)(2,1)S(1)} %slice.18), channel_id=1, source_target_pairs={{0,1},{1,2},{2,3},{3,0},{4,5},{5,6},{6,7},{7,4},{8,9},{9,10},{10,1... | collective-permute-start | bytes 1179656 | tf_op jit(solution)/shard_map/ppermute | solution.py:17
  136.7 10.5 %copy-start.3 = (bf16[512,768]{1,0:T(8,128)(2,1)}, bf16[512,768]{1,0:T(8,128)(2,1)S(1)}, u32[]{:S(2)}) copy-start(bf16[512,768]{1,0:T(8,128)(2,1)S(1)} %convolution_convert_fusion.1) | copy-start | bytes 2359300
  139.3 26.4 %collective-permute-start.18 = (bf16[768,512]{1,0:T(8,128)(2,1)S(1)}, bf16[768,512]{1,0:T(8,128)(2,1)}, u32[]{:S(2)}, u32[]{:S(2)}) collective-permute-start(bf16[768,512]{1,0:T(8,128)(2,1)S(1)} %get-tuple-element.25), channel_id=1, source_target_pairs={{0,128},{1,129},{2,130},{3,131},{36,132},{37,133},{38,134},{39,135... | collective-permute-start | bytes 2359304 | tf_op jit(solution)/shard_map/ppermute | solution.py:93
  140.8 24.8 %collective-permute-start.17 = (bf16[768,512]{1,0:T(8,128)(2,1)S(1)}, bf16[768,512]{1,0:T(8,128)(2,1)}, u32[]{:S(2)}, u32[]{:S(2)}) collective-permute-start(bf16[768,512]{1,0:T(8,128)(2,1)S(1)} %get-tuple-element.25), channel_id=1, source_target_pairs={{0,192},{1,193},{2,194},{3,195},{36,196},{37,197},{38,198},{39,199... | collective-permute-start | bytes 2359304 | tf_op jit(solution)/shard_map/ppermute | solution.py:93
  142.8 1.4 copy-start.2
  144.3 21.3 %collective-permute-start.16 = (bf16[768,512]{1,0:T(8,128)(2,1)S(1)}, bf16[768,512]{1,0:T(8,128)(2,1)}, u32[]{:S(2)}, u32[]{:S(2)}) collective-permute-start(bf16[768,512]{1,0:T(8,128)(2,1)S(1)} %get-tuple-element.25), channel_id=1, source_target_pairs={{0,64},{1,65},{2,66},{3,67},{36,68},{37,69},{38,70},{39,71},{72,13... | collective-permute-start | bytes 2359304 | tf_op jit(solution)/shard_map/ppermute | solution.py:93
  145.9 19.7 %collective-permute-start.22 = (bf16[768,512]{1,0:T(8,128)(2,1)}, bf16[768,512]{1,0:T(8,128)(2,1)S(1)}, u32[]{:S(2)}, u32[]{:S(2)}) collective-permute-start(bf16[768,512]{1,0:T(8,128)(2,1)} %get-tuple-element.24), channel_id=1, source_target_pairs={{0,32},{1,33},{2,34},{3,35},{36,4},{37,5},{38,6},{39,7},{72,104},{... | collective-permute-start | bytes 2359304 | tf_op jit(solution)/shard_map/ppermute | solution.py:93
  151.1 17.3 %collective-permute-start.14 = (bf16[512,768]{1,0:T(8,128)(2,1)}, bf16[512,768]{1,0:T(8,128)(2,1)}, u32[]{:S(2)}, u32[]{:S(2)}) collective-permute-start(bf16[512,768]{1,0:T(8,128)(2,1)} %get-tuple-element.40), channel_id=1, source_target_pairs={{0,32},{32,0},{1,33},{33,1},{2,34},{34,2},{3,35},{35,3},{4,36},{36... | collective-permute-start | bytes 2359304 | tf_op jit(solution)/shard_map/ppermute | solution.py:102
  165.6 2.8 %copy-start.4 = (bf16[512,768]{1,0:T(8,128)(2,1)S(1)}, bf16[512,768]{1,0:T(8,128)(2,1)}, u32[]{:S(2)}) copy-start(bf16[512,768]{1,0:T(8,128)(2,1)} %copy-done.3) | copy-start | bytes 2359300
  165.6 2.8 %copy-start.5 = (bf16[512,768]{1,0:T(8,128)(2,1)S(1)}, bf16[512,768]{1,0:T(8,128)(2,1)}, u32[]{:S(2)}) copy-start(bf16[512,768]{1,0:T(8,128)(2,1)} %get-tuple-element.41) | copy-start | bytes 2359300
  168.4 3.2 %copy-start.7 = (s32[2,48]{1,0:T(2,128)S(1)}, s32[2,48]{1,0:T(2,128)}, u32[]{:S(2)}) copy-start(s32[2,48]{1,0:T(2,128)} %param.5) | copy-start | bytes 1156
  169.9 51.7 %copy-start.6 = (f32[2,512,64]{1,2,0:T(8,128)S(1)}, f32[2,512,64]{1,2,0:T(8,128)}, u32[]{:S(2)}) copy-start(f32[2,512,64]{1,2,0:T(8,128)} %param.9) | copy-start | bytes 786436
  169.9 6.2 %collective-permute-start.23 = (bf16[128,768]{1,0:T(8,128)(2,1)S(1)}, bf16[128,768]{1,0:T(8,128)(2,1)S(1)}, u32[]{:S(2)}, u32[]{:S(2)}) collective-permute-start(bf16[128,768]{1,0:T(8,128)(2,1)S(1)} %get-tuple-element.26), channel_id=1, source_target_pairs={{0,128},{64,192},{128,0},{192,64},{1,129},{65,193},{129,1},{193,65... | collective-permute-start | bytes 589832 | tf_op jit(solution)/shard_map/ppermute | solution.py:17
  170.0 6.1 %collective-permute-start.25 = (bf16[128,768]{1,0:T(8,128)(2,1)S(1)}, bf16[128,768]{1,0:T(8,128)(2,1)S(1)}, u32[]{:S(2)}, u32[]{:S(2)}) collective-permute-start(bf16[128,768]{1,0:T(8,128)(2,1)S(1)} %get-tuple-element.27), channel_id=1, source_target_pairs={{0,192},{64,0},{128,64},{192,128},{1,193},{65,1},{129,65},{193,129... | collective-permute-start | bytes 589832 | tf_op jit(solution)/shard_map/ppermute | solution.py:17
  170.1 8.0 %collective-permute-start.24 = (bf16[128,768]{1,0:T(8,128)(2,1)S(1)}, bf16[128,768]{1,0:T(8,128)(2,1)S(1)}, u32[]{:S(2)}, u32[]{:S(2)}) collective-permute-start(bf16[128,768]{1,0:T(8,128)(2,1)S(1)} %get-tuple-element.28), channel_id=1, source_target_pairs={{0,64},{64,128},{128,192},{192,0},{1,65},{65,129},{129,193},{193,1... | collective-permute-start | bytes 589832 | tf_op jit(solution)/shard_map/ppermute | solution.py:17
  178.6 4.2 %collective-permute-start.27 = (bf16[32,512]{1,0:T(8,128)(2,1)S(1)}, bf16[32,512]{1,0:T(8,128)(2,1)S(1)}, u32[]{:S(2)}, u32[]{:S(2)}) collective-permute-start(bf16[32,512]{1,0:T(8,128)(2,1)S(1)} %get-tuple-element.37), channel_id=1, source_target_pairs={{0,1},{1,0},{2,3},{3,2},{4,5},{5,4},{6,7},{7,6},{8,9},{9,8},{10,11... | collective-permute-start | bytes 98312 | tf_op jit(solution)/shard_map/ppermute | solution.py:117
  178.9 4.2 %collective-permute-start.29 = (bf16[32,512]{1,0:T(8,128)(2,1)S(1)}, bf16[32,512]{1,0:T(8,128)(2,1)S(1)}, u32[]{:S(2)}, u32[]{:S(2)}) collective-permute-start(bf16[32,512]{1,0:T(8,128)(2,1)S(1)} %get-tuple-element.38), channel_id=1, source_target_pairs={{0,3},{1,2},{2,1},{3,0},{4,7},{5,6},{6,5},{7,4},{8,11},{9,10},{10,... | collective-permute-start | bytes 98312 | tf_op jit(solution)/shard_map/ppermute | solution.py:117
  181.7 4.3 %collective-permute-start.28 = (bf16[32,512]{1,0:T(8,128)(2,1)S(1)}, bf16[32,512]{1,0:T(8,128)(2,1)S(1)}, u32[]{:S(2)}, u32[]{:S(2)}) collective-permute-start(bf16[32,512]{1,0:T(8,128)(2,1)S(1)} %get-tuple-element.39), channel_id=1, source_target_pairs={{0,2},{1,3},{2,0},{3,1},{4,6},{5,7},{6,4},{7,5},{8,10},{9,11},{10,... | collective-permute-start | bytes 98312 | tf_op jit(solution)/shard_map/ppermute | solution.py:117
  186.7 19.1 %all-to-all-start.1 = ((bf16[8,32,512]{2,1,0:T(8,128)(2,1)}), bf16[8,32,512]{2,1,0:T(8,128)(2,1)S(1)}, u32[]{:S(2)}, u32[]{:S(2)}) async-start(bf16[8,32,512]{2,1,0:T(8,128)(2,1)} %broadcast_in_dim.65), calls=%async_computation.1 | async-start | bytes 524288 | tf_op jit(solution)/shard_map/all_to_all | solution.py:129
  196.5 6.6 %collective-permute-start.26 = (bf16[64,768]{1,0:T(8,128)(2,1)S(1)}, bf16[64,768]{1,0:T(8,128)(2,1)S(1)}, u32[]{:S(2)}, u32[]{:S(2)}) collective-permute-start(bf16[64,768]{1,0:T(8,128)(2,1)S(1)} %dynamic-slice_bitcast_fusion.3), channel_id=1, source_target_pairs={{0,32},{32,0},{1,33},{33,1},{2,34},{34,2},{3,35},{35,3},{4,36},{36... | collective-permute-start | bytes 294920 | tf_op jit(solution)/shard_map/ppermute | solution.py:143
  205.9 5.7 %collective-permute-start.32 = (bf16[32,512]{1,0:T(8,128)(2,1)S(1)}, bf16[32,512]{1,0:T(8,128)(2,1)S(1)}, u32[]{:S(2)}, u32[]{:S(2)}) collective-permute-start(bf16[32,512]{1,0:T(8,128)(2,1)S(1)} %reduce_sum.12), channel_id=1, source_target_pairs={{0,3},{1,2},{2,1},{3,0},{4,7},{5,6},{6,5},{7,4},{8,11},{9,10},{10,... | collective-permute-start | bytes 98312 | tf_op jit(solution)/shard_map/ppermute | solution.py:117
  206.5 5.1 %collective-permute-start.31 = (bf16[32,512]{1,0:T(8,128)(2,1)S(1)}, bf16[32,512]{1,0:T(8,128)(2,1)S(1)}, u32[]{:S(2)}, u32[]{:S(2)}) collective-permute-start(bf16[32,512]{1,0:T(8,128)(2,1)S(1)} %reduce_sum.12), channel_id=1, source_target_pairs={{0,2},{1,3},{2,0},{3,1},{4,6},{5,7},{6,4},{7,5},{8,10},{9,11},{10,... | collective-permute-start | bytes 98312 | tf_op jit(solution)/shard_map/ppermute | solution.py:117
  208.5 3.1 %collective-permute-start.30 = (bf16[32,512]{1,0:T(8,128)(2,1)S(1)}, bf16[32,512]{1,0:T(8,128)(2,1)S(1)}, u32[]{:S(2)}, u32[]{:S(2)}) collective-permute-start(bf16[32,512]{1,0:T(8,128)(2,1)S(1)} %reduce_sum.12), channel_id=1, source_target_pairs={{0,1},{1,0},{2,3},{3,2},{4,5},{5,4},{6,7},{7,6},{8,9},{9,8},{10,11... | collective-permute-start | bytes 98312 | tf_op jit(solution)/shard_map/ppermute | solution.py:117
  211.6 9.9 %collective-permute-start.33 = (bf16[64,512]{1,0:T(8,128)(2,1)S(1)}, bf16[64,512]{1,0:T(8,128)(2,1)S(1)}, u32[]{:S(2)}, u32[]{:S(2)}) collective-permute-start(bf16[64,512]{1,0:T(8,128)(2,1)S(1)} %dynamic-slice_bitcast_fusion.4), channel_id=1, source_target_pairs={{0,32},{32,0},{1,33},{33,1},{2,34},{34,2},{3,35},{35,3},{4,36},{36... | collective-permute-start | bytes 196616 | tf_op jit(solution)/shard_map/ppermute | solution.py:143
